TPU v7x, 128 devices: a whole 4x4x4 slice. The times are simulated.
128 devices in a mesh: seq: 16 (over z_lo, y, core), head: 8 (over z_hi, x).
Axes of the slice: x: 4, y: 4, z: 4 (z_hi: 2, z_lo: 2; z = z_hi * 2 + z_lo), core: 2. Of those that a mesh axis runs over, the one named last changes fastest.
Arguments:
- queries: bfloat16 [8192, 4096], P('seq', 'head'), may hold values from -6 to 6
- new_keys: bfloat16 [8192, 4096], P('seq', 'head'), may hold values from -6 to 6
- new_values: bfloat16 [8192, 4096], P('seq', 'head'), may hold values from -6 to 6
- pool_keys: bfloat16 [16384, 4096], P('seq', 'head'), may hold values from -6 to 6
- pool_values: bfloat16 [16384, 4096], P('seq', 'head'), may hold values from -6 to 6
- cache_len: int32 [4], replicated, may hold values from 128 to 4096, as said below
- cached_table: int32 [4, 32], replicated, may hold values from -1 to 127, as said below
- free_blocks: int32 [4, 16], replicated, may hold values from 0 to 127, as said below
- residual_in: bfloat16 [8192, 7168], P('seq', 'head'), may hold values from -26 to 26
- out_weight: bfloat16 [4096, 7168], P('head'), may hold values from -2.390625 to 2.390625
- out_bias: float32 [7168], P('head'), may hold values from -3 to 3
- ln_gain: float32 [7168], P('head'), may hold values from 0.1 to 1.9
- ln_bias: float32 [7168], P('head'), may hold values from -3 to 3
Outputs:
- hidden: bfloat16 [8192, 7168], P('seq', 'head')
- normed: bfloat16 [8192, 7168], P('seq', 'head')
- keys_out: bfloat16 [16384, 4096], P('seq', 'head')
- values_out: bfloat16 [16384, 4096], P('seq', 'head')
Inputs may be any that keep to these rules, and one draw needn't show every extreme that they name: `cache_len`: a multiple of 128; exactly one prompt has 4096 cached positions. `cached_table`: entry [p, j] names the pool block that holds cached positions j * 128 to j * 128 + 127 of prompt p when j < cache_len[p] / 128, and is -1 otherwise; the named blocks are all different and lie anywhere in the pool. `free_blocks`: all different and never named by cached_table; block free_blocks[p, j] lies in the pool rows held by the same index of seq as token row p * 2048 + j * 128, that is free_blocks[p, j] * 128 // 1024 == (p * 2048 + j * 128) // 512.
All inputs are finite; a program needn't handle non-finite values.
Results may differ from a plain program's by a relative error of at most 0.022.
Values may be sent and summed in bfloat16 or wider, within the bound.
No kernel may reach another device: no remote copies, remote signals or barrier semaphores. Data moves between devices by JAX's collectives and lax.ppermute only.
A program may use at most 384 MiB of HBM per device.

v0:
```python
import jax
import jax.numpy as jnp
from jax import lax
from jax.sharding import PartitionSpec as P

D = 7168
HD = 128
NEW_LEN = 2048
BLOCK = 128
NEGATIVE = -1e30


def key_facts(block_count, cached_table, free_blocks, cache_len):
    block_ids = jnp.arange(block_count, dtype=jnp.int32)
    prompt_count, cached_count = cached_table.shape
    fresh_count = free_blocks.shape[1]
    prompt_ids = jnp.arange(prompt_count, dtype=jnp.int32)
    in_cache = cached_table[None, :, :] == block_ids[:, None, None]
    in_fresh = free_blocks[None, :, :] == block_ids[:, None, None]
    owner = jnp.sum(jnp.where(in_cache, prompt_ids[None, :, None] + 1, 0), axis=(1, 2))
    owner = owner + jnp.sum(jnp.where(in_fresh, prompt_ids[None, :, None] + 1, 0), axis=(1, 2)) - 1
    cached_slot = jnp.arange(cached_count, dtype=jnp.int32)
    fresh_slot = (cache_len // BLOCK)[:, None] + jnp.arange(fresh_count, dtype=jnp.int32)[None, :]
    logical = jnp.sum(jnp.where(in_cache, cached_slot[None, None, :], 0), axis=(1, 2))
    logical = logical + jnp.sum(jnp.where(in_fresh, fresh_slot[None, :, :], 0), axis=(1, 2))
    key_owner = jnp.repeat(owner, BLOCK)
    key_place = (logical[:, None] * BLOCK + jnp.arange(BLOCK, dtype=jnp.int32)[None, :]).reshape(-1)
    return (key_owner, key_place)


def query_facts(first_row, row_count, cache_len):
    rows = first_row + jnp.arange(row_count, dtype=jnp.int32)
    owner = rows // NEW_LEN
    place = rows % NEW_LEN
    prompt_ids = jnp.arange(cache_len.shape[0], dtype=jnp.int32)
    limit = (
        jnp.sum(jnp.where(owner[:, None] == prompt_ids[None, :], cache_len[None, :], 0), axis=1)
        + place
    )
    return (owner, limit)


def attend(query_rows, query_owner, query_limit, keys, values, key_owner, key_place):
    row_count = query_rows.shape[0]
    heads_here = query_rows.shape[1] // HD
    key_count = keys.shape[0]
    query_split = query_rows.reshape(row_count, heads_here, HD)
    key_split = keys.reshape(key_count, heads_here, HD)
    value_split = values.reshape(key_count, heads_here, HD)
    visible = (key_owner[None, :] == query_owner[:, None]) & (
        key_place[None, :] <= query_limit[:, None]
    )
    scores = jnp.einsum(
        "rhd,khd->hrk", query_split, key_split, preferred_element_type=jnp.float32
    ) * HD ** (-0.5)
    scores = jnp.where(visible[None, :, :], scores, NEGATIVE)
    peak = jnp.max(scores, axis=2)
    weights = jnp.where(visible[None, :, :], jnp.exp(scores - peak[:, :, None]), 0.0)
    total = jnp.sum(weights, axis=2)
    mixed = jnp.einsum(
        "hrk,khd->rhd",
        weights.astype(jnp.bfloat16),
        value_split,
        preferred_element_type=jnp.float32,
    )
    return (peak.T, total.T, mixed.reshape(row_count, heads_here * HD))


def combine(first, second):
    peak = jnp.maximum(first[0], second[0])
    scale_first = jnp.exp(first[0] - peak)
    scale_second = jnp.exp(second[0] - peak)
    total = second[1] * scale_second
    row_count, heads_here = peak.shape
    mixed = first[2].reshape(row_count, heads_here, HD) * scale_first[:, :, None]
    mixed = second[2].reshape(row_count, heads_here, HD) * scale_second[:, :, None]
    return (peak, total, mixed.reshape(row_count, heads_here * HD))


def shards(
    queries,
    new_keys,
    new_values,
    pool_keys,
    pool_values,
    cache_len,
    cached_table,
    free_blocks,
    residual_in,
    out_weight,
    out_bias,
    ln_gain,
    ln_bias,
):
    token_rows, width = queries.shape
    heads_here = width // HD
    pool_rows = pool_keys.shape[0]
    per_device = pool_rows // BLOCK
    fresh_device = token_rows // BLOCK
    position = lax.axis_index("seq")
    first_row = position * token_rows
    prompt_here = first_row // NEW_LEN
    first_slot = first_row % NEW_LEN // BLOCK
    targets = (
        lax.dynamic_slice(free_blocks, (prompt_here, first_slot), (1, fresh_device))[0]
        - position * per_device
    )
    keys_out = (
        pool_keys.reshape(per_device, BLOCK, width)
        .at[targets]
        .set(new_keys.reshape(fresh_device, BLOCK, width))
        .reshape(pool_rows, width)
    )
    values_out = (
        pool_values.reshape(per_device, BLOCK, width)
        .at[targets]
        .set(new_values.reshape(fresh_device, BLOCK, width))
        .reshape(pool_rows, width)
    )
    own_owner, own_limit = query_facts(first_row, token_rows, cache_len)
    start_state = (
        jnp.full((token_rows, heads_here), NEGATIVE, jnp.float32),
        jnp.zeros((token_rows, heads_here), jnp.float32),
        jnp.zeros((token_rows, width), jnp.float32),
    )
    piece_keys = lax.all_gather(keys_out, "seq", axis=0, tiled=True)
    piece_values = lax.all_gather(values_out, "seq", axis=0, tiled=True)
    key_owner, key_place = key_facts(
        piece_keys.shape[0] // BLOCK, cached_table, free_blocks, cache_len
    )
    peak, total, mixed = combine(
        start_state,
        attend(queries, own_owner, own_limit, piece_keys, piece_values, key_owner, key_place),
    )
    attn = (
        (mixed.reshape(token_rows, heads_here, HD) / total[:, :, None])
        .reshape(token_rows, width)
        .astype(jnp.bfloat16)
    )
    projected = jnp.dot(attn, out_weight, preferred_element_type=jnp.float32)
    summed = lax.psum_scatter(
        projected.astype(jnp.bfloat16), "head", scatter_dimension=1, tiled=True
    ).astype(jnp.float32)
    stream = residual_in.astype(jnp.float32) + summed + out_bias[None, :]
    mean = lax.psum(jnp.sum(stream, axis=1), "head") / D
    centred = stream - mean[:, None]
    variance = lax.psum(jnp.sum(centred * centred, axis=1), "head") / D
    normed = (
        centred * lax.rsqrt(variance[:, None] + 1e-05) * ln_gain[None, :] + ln_bias[None, :]
    ).astype(jnp.bfloat16)
    return (stream.astype(jnp.bfloat16), normed, keys_out, values_out)


def solution(mesh):
    in_specs = (
        P("seq", "head"),
        P("seq", "head"),
        P("seq", "head"),
        P("seq", "head"),
        P("seq", "head"),
        P(),
        P(),
        P(),
        P("seq", "head"),
        P("head", None),
        P("head"),
        P("head"),
        P("head"),
    )
    out_specs = (P("seq", "head"), P("seq", "head"), P("seq", "head"), P("seq", "head"))
    return jax.shard_map(shards, mesh=mesh, in_specs=in_specs, out_specs=out_specs, check_vma=False)
```

profile of v0, /device:TPU:0, one launch (start us, length us, event | category | flops | bytes accessed | tf_op | source)
XLA Modules:
  0.0 465.4 jit_solution(8003422405766926117)
XLA Ops:
  7.2 0.0 copy-start
  7.2 0.0 all-gather.5.cloned.1.call-start
  7.2 1.3 copy.59
  8.5 1.2 copy.60
  9.7 0.8 fusion.22
  10.5 1.7 scatter_fusion.1
  12.2 0.0 copy-start.4
  12.2 1.3 copy.38
  13.5 0.0 all-gather.5.cloned.1.call-update
  13.5 0.0 all-gather.3.cloned.1.call-start
  13.6 1.7 scatter_fusion
  15.3 0.0 copy-start.3
  15.3 1.0 copy-done.3
  16.3 0.0 all-gather.3.cloned.1.call-update
  16.3 0.0 reduce-scatter.4.cloned.1.call-start
  16.4 0.7 select_reduce_fusion.4
  17.1 0.8 select_reduce_fusion.1
  17.9 0.7 and_select_fusion
  18.6 0.1 iota_add_fusion
  18.6 0.8 select_reduce_fusion.3
  19.4 0.1 add_bitcast_fusion
  19.5 0.1 broadcast_bitcast_fusion
  19.6 13.3 %compare_and_fusion = pred[512,16384]{0,1:T(8,128)(4,1)} fusion(s32[512]{0:T(512)S(1)} %fusion.18, s32[512]{0:T(512)S(1)} %add_select_fusion.1, s32[16384]{0:T(1024)S(1)} %add_bitcast_fusion, s32[16384]{0:T(1024)S(1)} %broadcast_bitcast_fusion), kind=kLoop, calls=%fused_computation.9 | loop fusion | flops 25165824 | bytes 8523776 | tf_op jit(solution)/shard_map/and | solution.py:50
  32.9 74.9 %all-gather.5.cloned.1.call-done = bf16[16384,512]{0,1:T(8,128)(2,1)} async-done(((bf16[1024,512]{0,1:T(8,128)(2,1)}), bf16[16384,512]{0,1:T(8,128)(2,1)}) %all-gather.5.cloned.1.call-update) | async-done | bytes 16777232 | tf_op jit(solution)/shard_map/all_gather | solution.py:126
  107.8 0.0 copy-done
  107.8 59.0 %fusion = (f32[4,512]{1,0:T(4,128)S(1)}, f32[4,16384,512]{2,1,0:T(8,128)}) fusion(pred[512,16384]{0,1:T(8,128)(4,1)} %compare_and_fusion, bf16[16384,4,128]{0,2,1:T(8,128)(2,1)} %bitcast.79, bf16[512,512]{1,0:T(8,128)(2,1)S(1)} %copy-done), kind=kOutput, calls=%fused_computation.4 | convolution fusion | flops 8690595840 | bytes 159916032 | tf_op jit(solution)/shard_map/rhd,khd->hrk/dot_general | solution.py:53
  166.8 0.0 copy-done.4
  166.8 45.4 %fusion.1 = f32[4,512]{1,0:T(4,128)S(1)} fusion(f32[4,16384,512]{2,1,0:T(8,128)} %get-tuple-element.17, f32[4,512]{1,0:T(4,128)S(1)} %get-tuple-element.16, pred[512,16384]{0,1:T(8,128)(4,1)} %compare_and_fusion), kind=kLoop, calls=%fused_computation.5 | loop fusion | flops 167770112 | bytes 142622720 | tf_op jit(solution)/shard_map/reduce_sum | solution.py:59
  212.2 0.0 all-gather.3.cloned.1.call-done
  212.2 21.3 %copy.37 = bf16[16384,512]{0,1:T(8,128)(2,1)} copy(bf16[16384,512]{1,0:T(8,128)(2,1)} %all-gather.3.cloned.1.call-done) | data formatting | bytes 33554432 | tf_op jit(solution)/shard_map/all_gather | solution.py:127
  233.5 52.8 %divide_convert_fusion = bf16[512,4,128]{0,2,1:T(8,128)(2,1)S(1)} fusion(f32[512,4]{0,1:T(4,128)S(1)} %get-tuple-element.14, f32[512,4]{0,1:T(4,128)S(1)} %get-tuple-element.15, bf16[16384,4,128]{0,2,1:T(8,128)(2,1)} %bitcast.68, f32[4,16384,512]{2,1,0:T(8,128)} %get-tuple-element.17, f32[4,512]{1,0:T(4,128)S(1)} %get-tuple-element.16, ...), kind=kOutput, calls=%fused_computation.18 | convolution fusion | flops 8758493184 | bytes 159932416 | tf_op jit(solution)/shard_map/hrk,khd->rhd/dot_general | solution.py:60
  286.3 0.0 copy-start.2
  286.3 0.0 copy-start.5
  286.3 0.0 copy-start.1
  286.3 9.5 %convolution_convert_fusion = bf16[512,7168]{1,0:T(8,128)(2,1)} fusion(bf16[512,512]{0,1:T(8,128)(2,1)S(1)} %bitcast.78, bf16[512,7168]{1,0:T(8,128)(2,1)} %param.22), kind=kOutput, calls=%fused_computation.10 | convolution fusion | flops 3761766400 | bytes 15204352 | tf_op jit(solution)/shard_map/dot_general | solution.py:140
  295.9 0.0 copy-start.6
  295.9 0.0 copy-start.7
  295.9 10.4 %copy.44 = bf16[512,7168]{0,1:T(8,128)(2,1)} copy(bf16[512,7168]{1,0:T(8,128)(2,1)} %convolution_convert_fusion) | data formatting | bytes 14680064
  306.3 0.0 reduce-scatter.4.cloned.1.call-update
  306.3 108.4 %reduce-scatter.4.cloned.1.call-done = bf16[896,512]{1,0:T(8,128)(2,1)} async-done(((bf16[7168,512]{1,0:T(8,128)(2,1)}), bf16[896,512]{1,0:T(8,128)(2,1)}) %reduce-scatter.4.cloned.1.call-update) | async-done | bytes 917520
  414.7 1.5 copy.45
  416.3 0.0 copy-done.2
  416.3 0.0 copy-done.5
  416.3 0.4 fusion.12
  416.7 20.3 %psum.14 = f32[512]{0:T(512)S(1)} all-reduce(f32[512]{0:T(512)S(1)} %fusion.12), channel_id=1, replica_groups=mesh['seq'=16,'head'=8] {'head'}, use_global_device_ids=true, to_apply=%region_11.12 | all-reduce | flops 512 | bytes 4096 | tf_op jit(solution)/shard_map/psum | solution.py:145
  437.0 0.5 multiply_reduce_fusion
  437.5 19.6 %psum.15 = f32[512]{0:T(512)S(1)} all-reduce(f32[512]{0:T(512)S(1)} %multiply_reduce_fusion), channel_id=1, replica_groups=mesh['seq'=16,'head'=8] {'head'}, use_global_device_ids=true, to_apply=%region_13.14 | all-reduce | flops 512 | bytes 4096 | tf_op jit(solution)/shard_map/psum | solution.py:147
  457.1 0.0 copy-done.6
  457.1 0.0 copy-done.7
  457.1 1.8 add_convert_fusion
  458.9 0.0 copy-done.1
  (7 shorter events, 0.1 us)
Async XLA Ops:
  7.2 100.6 %copy-start = (bf16[512,512]{1,0:T(8,128)(2,1)S(1)}, bf16[512,512]{1,0:T(8,128)(2,1)}, u32[]{:S(2)}) copy-start(bf16[512,512]{1,0:T(8,128)(2,1)} %param.13) | copy-start | bytes 1572868
  7.2 100.6 %all-gather.5.cloned.1.call-start = ((), (), s32[]{:S(2)}) async-start(), calls=%async_computation.2 | async-start | bytes 17825792 | tf_op jit(solution)/shard_map/all_gather | solution.py:126
  12.2 154.6 %copy-start.4 = (bf16[8,128,512]{2,1,0:T(8,128)(2,1)}, bf16[8,128,512]{2,1,0:T(8,128)(2,1)S(1)}, u32[]{:S(2)}) copy-start(bf16[8,128,512]{2,1,0:T(8,128)(2,1)S(1)} %scatter_fusion.1) | copy-start | bytes 3145732
  13.5 198.6 %all-gather.3.cloned.1.call-start = ((), (), s32[]{:S(2)}) async-start(), calls=%async_computation.1 | async-start | bytes 17825792 | tf_op jit(solution)/shard_map/all_gather | solution.py:127
  15.3 1.0 copy-start.3
  16.3 398.4 %reduce-scatter.4.cloned.1.call-start = ((), (), s32[]{:S(2)}) async-start(), calls=%async_computation.3 | async-start | bytes 8257536
  286.3 130.0 %copy-start.2 = (bf16[512,896]{1,0:T(8,128)(2,1)S(1)}, bf16[512,896]{1,0:T(8,128)(2,1)}, u32[]{:S(2)}) copy-start(bf16[512,896]{1,0:T(8,128)(2,1)} %param.21) | copy-start | bytes 2752516
  286.3 130.0 %copy-start.5 = (f32[896]{0:T(1024)S(1)}, f32[896]{0:T(1024)}, u32[]{:S(2)}) copy-start(f32[896]{0:T(1024)} %param.23) | copy-start | bytes 10756
  286.3 172.6 %copy-start.1 = (bf16[512,512]{1,0:T(8,128)(2,1)S(1)}, bf16[512,512]{1,0:T(8,128)(2,1)}, u32[]{:S(2)}) copy-start(bf16[512,512]{1,0:T(8,128)(2,1)} %param.13) | copy-start | bytes 1572868
  295.9 161.2 %copy-start.6 = (f32[896]{0:T(1024)S(1)}, f32[896]{0:T(1024)}, u32[]{:S(2)}) copy-start(f32[896]{0:T(1024)} %param.25) | copy-start | bytes 10756
  295.9 161.2 %copy-start.7 = (f32[896]{0:T(1024)S(1)}, f32[896]{0:T(1024)}, u32[]{:S(2)}) copy-start(f32[896]{0:T(1024)} %param.24) | copy-start | bytes 10756
Sparse Core Ops, SparseCore 0:
  13.7 94.0 all-gather.4
  110.1 92.4 all-gather.2
  306.5 108.2 reduce-scatter.3
where the time goes:
time: 467 us; the launch traced here: 465 us
  waiting for transfers between devices  183 us (39%)
  matrix products  121 us (26%)
  other arithmetic  65.2 us (14%)
  local copies, waits for them, and re-layouts  41.5 us (9%)
  blocking collectives  39.9 us (9%)
  between operations  13.9 us (3%)
    unnamed x4, waiting for transfers between devices  108 us
    all_gather x1, waiting for transfers between devices, shards(): piece_keys = lax.all_gather(keys_out, 'seq', axis=0, tiled=True)  74.9 us
    dot_general x1, matrix products, attend(): jnp.einsum('rhd,khd->hrk', query_split, key_split, preferred_element_type...  59 us
    dot_general x1, matrix products, attend(): jnp.einsum('hrk,khd->rhd', weights.astype(jnp.bfloat16), value_split, pre...  52.8 us
    reduce_sum x1, other arithmetic, attend(): total = jnp.sum(weights, axis=2)  45.4 us
    all_gather x1, local copies, waits for them, and re-layouts, shards(): piece_values = lax.all_gather(values_out, 'seq', axis=0, tiled=True)  21.3 us
    psum x1, blocking collectives, shards(): mean = lax.psum(jnp.sum(stream, axis=1), 'head') / D  20.3 us
    psum x1, blocking collectives, shards(): variance = lax.psum(jnp.sum(centred * centred, axis=1), 'head') / D  19.6 us
  transfers between devices with their start and end apart: 3, of which 2 were waited for; matrix products, arithmetic and copies ran while one was open for 26% of the time, Pallas kernels for 0%

commit v1 on v0

--- a/solution.py
+++ b/solution.py
@@ -123,7 +123,9 @@
         jnp.zeros((token_rows, heads_here), jnp.float32),
         jnp.zeros((token_rows, width), jnp.float32),
     )
-    piece_keys = lax.all_gather(keys_out, "seq", axis=0, tiled=True)
+    piece_keys = jnp.concatenate(
+        lax.all_to_all(jnp.stack([keys_out] * lax.axis_size("seq")), "seq", 0, 0), axis=0
+    )
     piece_values = lax.all_gather(values_out, "seq", axis=0, tiled=True)
     key_owner, key_place = key_facts(
         piece_keys.shape[0] // BLOCK, cached_table, free_blocks, cache_len

time: 467 us -> 711 us (1.52)
  waiting for transfers between devices: 183 us -> 381 us
  local copies, waits for them, and re-layouts: 41.5 us -> 89 us
    all_to_all x0 -> x1, waiting for transfers between devices: none -> 271 us  [shards(): lax.all_to_all(jnp.stack([keys_out] * lax.axis_size('seq')), 'seq', 0, 0)]
    all_gather x1 -> x0, waiting for transfers between devices: 74.9 us -> none  [shards(): piece_keys = lax.all_gather(keys_out, 'seq', axis=0, tiled=True)]
    another operation x0 -> x3, local copies, waits for them, and re-layouts: none -> 32.3 us  [the longest x1 25.6 us: attend(): key_split = keys.reshape(key_count, heads_here, HD)]
    all_to_all x0 -> x1, local copies, waits for them, and re-layouts: none -> 18.7 us  [shards(): lax.all_to_all(jnp.stack([keys_out] * lax.axis_size('seq')), 'seq', 0, 0)]
    unnamed x20 -> x29, local copies, waits for them, and re-layouts: 15.5 us -> 14.3 us
    unnamed x4 -> x3, waiting for transfers between devices: 108 us -> 110 us
  transfers between devices with their start and end apart: 3 -> 3, of which waited for: 2 -> 2; matrix products, arithmetic and copies ran while one was open for 26% -> 22% of each run, Pallas kernels for 0% -> 0%
where the time goes in v1:
time: 711 us; the launch traced here: 709 us
  waiting for transfers between devices  381 us (54%)
  matrix products  118 us (17%)
  local copies, waits for them, and re-layouts  89 us (13%)
  other arithmetic  61 us (9%)
  blocking collectives  39.9 us (6%)
  between operations  14.3 us (2%)
    all_to_all x1, waiting for transfers between devices, shards(): lax.all_to_all(jnp.stack([keys_out] * lax.axis_size('seq')), 'seq', 0, 0)  271 us
    unnamed x3, waiting for transfers between devices  110 us
    dot_general x1, matrix products, attend(): jnp.einsum('rhd,khd->hrk', query_split, key_split, preferred_element_type...  55.8 us
    dot_general x1, matrix products, attend(): jnp.einsum('hrk,khd->rhd', weights.astype(jnp.bfloat16), value_split, pre...  52.8 us
    reduce_sum x1, other arithmetic, attend(): total = jnp.sum(weights, axis=2)  43.7 us
    another operation x1, local copies, waits for them, and re-layouts, attend(): key_split = keys.reshape(key_count, heads_here, HD)  25.6 us
    all_gather x1, local copies, waits for them, and re-layouts, shards(): piece_values = lax.all_gather(values_out, 'seq', axis=0, tiled=True)  21.3 us
    psum x1, blocking collectives, shards(): mean = lax.psum(jnp.sum(stream, axis=1), 'head') / D  20.3 us
  transfers between devices with their start and end apart: 3, of which 2 were waited for; matrix products, arithmetic and copies ran while one was open for 22% of the time, Pallas kernels for 0%

profile of v1, /device:TPU:0, one launch (start us, length us, event | category | flops | bytes accessed | tf_op | source)
XLA Modules:
  0.0 708.9 jit_solution(4044138878841472793)
XLA Ops:
  7.2 0.0 copy-start
  7.2 1.3 copy.54
  8.5 0.8 fusion.22
  9.2 1.7 scatter_fusion.1
  10.9 0.0 copy-start.5
  10.9 0.5 copy.32
  11.5 6.1 stack.3
  17.6 0.0 copy-start.4
  17.6 0.0 copy-start.6
  17.6 0.0 copy-start.12
  17.6 0.0 copy-start.11
  17.6 0.0 copy-start.10
  17.6 0.0 copy-done.5
  17.7 6.2 all-to-all-start
  23.9 0.0 all-gather.2.cloned.1.call-start
  23.9 0.0 copy-done.4
  23.9 0.0 copy-done.6
  23.9 0.7 scatter_fusion
  24.6 0.0 copy-start.3
  24.6 1.0 copy-done.3
  25.6 0.0 all-gather.2.cloned.1.call-update
  25.6 0.0 reduce-scatter.4.cloned.1.call-start
  25.7 0.0 copy-done.12
  25.7 0.1 select_reduce_fusion.4
  25.8 0.0 copy-done.11
  25.8 0.1 select_reduce_fusion.1
  25.9 0.1 iota_add_fusion
  26.0 0.0 copy-done.10
  26.0 0.1 select_reduce_fusion.3
  26.1 0.1 add_bitcast_fusion
  26.2 0.1 broadcast_bitcast_fusion
  26.3 13.3 %compare_and_fusion = pred[512,16384]{0,1:T(8,128)(4,1)} fusion(s32[512]{0:T(512)S(1)} %fusion.18, s32[512]{0:T(512)S(1)} %add_select_fusion.1, s32[16384]{0:T(1024)S(1)} %add_bitcast_fusion, s32[16384]{0:T(1024)S(1)} %broadcast_bitcast_fusion), kind=kLoop, calls=%fused_computation.9 | loop fusion | flops 25165824 | bytes 8523776 | tf_op jit(solution)/shard_map/and | solution.py:50
  39.6 270.9 %all-to-all-done = bf16[16,1024,512]{1,2,0:T(8,128)(2,1)} async-done(((bf16[16,1024,512]{1,2,0:T(8,128)(2,1)}), bf16[16,1024,512]{1,2,0:T(8,128)(2,1)}, u32[]{:S(2)}, u32[]{:S(2)}) %all-to-all-start) | async-done | bytes 16777248 | tf_op jit(solution)/shard_map/all_to_all | solution.py:127
  310.5 18.7 %copy.33 = bf16[16,1024,512]{1,0,2:T(8,128)(2,1)} copy(bf16[16,1024,512]{1,2,0:T(8,128)(2,1)} %all-to-all-done) | data formatting | bytes 33554432 | tf_op jit(solution)/shard_map/all_to_all | solution.py:127
  329.2 25.6 %reshape_reshape.3 = bf16[16384,4,128]{0,2,1:T(8,128)(2,1)} reshape(bf16[16,1024,512]{1,0,2:T(8,128)(2,1)} %copy.33) | data formatting | bytes 33554432 | tf_op jit(solution)/shard_map/reshape;reshape | solution.py:48
  354.8 0.0 copy-done
  354.8 55.8 %fusion = (f32[4,512]{1,0:T(4,128)S(1)}, f32[4,16384,512]{2,1,0:T(8,128)}) fusion(pred[512,16384]{0,1:T(8,128)(4,1)} %compare_and_fusion, bf16[16384,4,128]{0,2,1:T(8,128)(2,1)} %reshape_reshape.3, bf16[512,512]{1,0:T(8,128)(2,1)S(1)} %copy-done), kind=kOutput, calls=%fused_computation.4 | convolution fusion | flops 8690595840 | bytes 159916032 | tf_op jit(solution)/shard_map/rhd,khd->hrk/dot_general | solution.py:53
  410.6 43.7 %fusion.1 = f32[4,512]{1,0:T(4,128)S(1)} fusion(f32[4,16384,512]{2,1,0:T(8,128)} %get-tuple-element.13, f32[4,512]{1,0:T(4,128)S(1)} %get-tuple-element.12, pred[512,16384]{0,1:T(8,128)(4,1)} %compare_and_fusion), kind=kLoop, calls=%fused_computation.5 | loop fusion | flops 167770112 | bytes 142622720 | tf_op jit(solution)/shard_map/reduce_sum | solution.py:59
  454.4 0.0 all-gather.2.cloned.1.call-done
  454.4 21.3 %copy.31 = bf16[16384,512]{0,1:T(8,128)(2,1)} copy(bf16[16384,512]{1,0:T(8,128)(2,1)} %all-gather.2.cloned.1.call-done) | data formatting | bytes 33554432 | tf_op jit(solution)/shard_map/all_gather | solution.py:129
  475.7 52.8 %divide_convert_fusion = bf16[512,4,128]{0,2,1:T(8,128)(2,1)S(1)} fusion(f32[512,4]{0,1:T(4,128)S(1)} %get-tuple-element.10, f32[512,4]{0,1:T(4,128)S(1)} %get-tuple-element.11, bf16[16384,4,128]{0,2,1:T(8,128)(2,1)} %bitcast.69, f32[4,16384,512]{2,1,0:T(8,128)} %get-tuple-element.13, f32[4,512]{1,0:T(4,128)S(1)} %get-tuple-element.12, ...), kind=kOutput, calls=%fused_computation.18 | convolution fusion | flops 8758493184 | bytes 159932416 | tf_op jit(solution)/shard_map/hrk,khd->rhd/dot_general | solution.py:60
  528.5 0.0 copy-start.2
  528.5 0.0 copy-start.7
  528.5 0.0 copy-start.1
  528.5 9.3 %convolution_convert_fusion = bf16[512,7168]{1,0:T(8,128)(2,1)} fusion(bf16[512,512]{0,1:T(8,128)(2,1)S(1)} %bitcast.79, bf16[512,7168]{1,0:T(8,128)(2,1)} %param.22), kind=kOutput, calls=%fused_computation.10 | convolution fusion | flops 3761766400 | bytes 15204352 | tf_op jit(solution)/shard_map/dot_general | solution.py:142
  537.9 0.0 copy-start.8
  537.9 0.0 copy-start.9
  537.9 10.4 %copy.39 = bf16[512,7168]{0,1:T(8,128)(2,1)} copy(bf16[512,7168]{1,0:T(8,128)(2,1)} %convolution_convert_fusion) | data formatting | bytes 14680064
  548.3 0.0 reduce-scatter.4.cloned.1.call-update
  548.3 109.6 %reduce-scatter.4.cloned.1.call-done = bf16[896,512]{1,0:T(8,128)(2,1)} async-done(((bf16[7168,512]{1,0:T(8,128)(2,1)}), bf16[896,512]{1,0:T(8,128)(2,1)}) %reduce-scatter.4.cloned.1.call-update) | async-done | bytes 917520
  657.9 1.5 copy.40
  659.4 0.0 copy-done.2
  659.5 0.0 copy-done.7
  659.5 0.4 fusion.12
  659.8 20.3 %psum.14 = f32[512]{0:T(512)S(1)} all-reduce(f32[512]{0:T(512)S(1)} %fusion.12), channel_id=1, replica_groups=mesh['seq'=16,'head'=8] {'head'}, use_global_device_ids=true, to_apply=%region_11.12 | all-reduce | flops 512 | bytes 4096 | tf_op jit(solution)/shard_map/psum | solution.py:147
  680.2 0.5 multiply_reduce_fusion
  680.7 19.6 %psum.15 = f32[512]{0:T(512)S(1)} all-reduce(f32[512]{0:T(512)S(1)} %multiply_reduce_fusion), channel_id=1, replica_groups=mesh['seq'=16,'head'=8] {'head'}, use_global_device_ids=true, to_apply=%region_13.14 | all-reduce | flops 512 | bytes 4096 | tf_op jit(solution)/shard_map/psum | solution.py:149
  700.3 0.0 copy-done.8
  700.3 0.0 copy-done.9
  700.3 1.8 add_convert_fusion
  702.1 0.0 copy-done.1
  (8 shorter events, 0.1 us)
Async XLA Ops:
  7.2 347.6 %copy-start = (bf16[512,512]{1,0:T(8,128)(2,1)S(1)}, bf16[512,512]{1,0:T(8,128)(2,1)}, u32[]{:S(2)}) copy-start(bf16[512,512]{1,0:T(8,128)(2,1)} %param.13) | copy-start | bytes 1572868
  10.9 6.7 copy-start.5
  17.6 6.3 copy-start.4
  17.6 6.3 copy-start.6
  17.6 8.1 %copy-start.12 = (s32[4]{0:T(128)S(1)}, s32[4]{0:T(128)}, u32[]{:S(2)}) copy-start(s32[4]{0:T(128)} %param.18) | copy-start | bytes 52
  17.6 8.2 %copy-start.11 = (s32[4,32]{1,0:T(4,128)S(1)}, s32[4,32]{1,0:T(4,128)}, u32[]{:S(2)}) copy-start(s32[4,32]{1,0:T(4,128)} %param.19) | copy-start | bytes 1540
  17.6 8.4 %copy-start.10 = (s32[4,16]{1,0:T(4,128)S(1)}, s32[4,16]{1,0:T(4,128)}, u32[]{:S(2)}) copy-start(s32[4,16]{1,0:T(4,128)} %param.20) | copy-start | bytes 772
  17.7 292.9 %all-to-all-start = ((bf16[16,1024,512]{1,2,0:T(8,128)(2,1)}), bf16[16,1024,512]{1,2,0:T(8,128)(2,1)}, u32[]{:S(2)}, u32[]{:S(2)}) async-start(bf16[16,1024,512]{1,2,0:T(8,128)(2,1)} %stack.3), calls=%async_computation | async-start | bytes 33554432 | tf_op jit(solution)/shard_map/all_to_all | solution.py:127
  23.9 430.5 %all-gather.2.cloned.1.call-start = ((), (), s32[]{:S(2)}) async-start(), calls=%async_computation.2 | async-start | bytes 17825792 | tf_op jit(solution)/shard_map/all_gather | solution.py:129
  24.6 1.0 copy-start.3
  25.6 632.3 %reduce-scatter.4.cloned.1.call-start = ((), (), s32[]{:S(2)}) async-start(), calls=%async_computation.3 | async-start | bytes 8257536
  528.5 131.0 %copy-start.2 = (bf16[512,896]{1,0:T(8,128)(2,1)S(1)}, bf16[512,896]{1,0:T(8,128)(2,1)}, u32[]{:S(2)}) copy-start(bf16[512,896]{1,0:T(8,128)(2,1)} %param.21) | copy-start | bytes 2752516
  528.5 131.0 %copy-start.7 = (f32[896]{0:T(1024)S(1)}, f32[896]{0:T(1024)}, u32[]{:S(2)}) copy-start(f32[896]{0:T(1024)} %param.23) | copy-start | bytes 10756
  528.5 173.6 %copy-start.1 = (bf16[512,512]{1,0:T(8,128)(2,1)S(1)}, bf16[512,512]{1,0:T(8,128)(2,1)}, u32[]{:S(2)}) copy-start(bf16[512,512]{1,0:T(8,128)(2,1)} %param.13) | copy-start | bytes 1572868
  537.9 162.4 %copy-start.8 = (f32[896]{0:T(1024)S(1)}, f32[896]{0:T(1024)}, u32[]{:S(2)}) copy-start(f32[896]{0:T(1024)} %param.25) | copy-start | bytes 10756
  537.9 162.4 %copy-start.9 = (f32[896]{0:T(1024)S(1)}, f32[896]{0:T(1024)}, u32[]{:S(2)}) copy-start(f32[896]{0:T(1024)} %param.24) | copy-start | bytes 10756
Sparse Core Ops, SparseCore 0:
  27.0 279.2 all-gather.1
  548.5 109.3 reduce-scatter.3
